TPU v7x, 512 devices: a whole 4x4x16 slice. The times are simulated.
512 devices in a mesh: blk: 32 (over y, x, core), int: 16 (over z).
Axes of the slice: x: 4, y: 4, z: 16, core: 2. Of those that a mesh axis runs over, the one named last changes fastest.
Arguments:
- amplitudes: float32 [4, 608, 64, 608], P(None, 'blk', 'int'), may hold values from -6 to 6
- integrals: float32 [64, 608, 4, 608], P('int', None, None, 'blk'), may hold values from -0.078125 to 0.078125
- occ_irrep: int32 [64], replicated, may hold values from 0 to 7
- virt_irrep: int32 [608], replicated, may hold values from 0 to 7, as said below
- i_batch: int32 [4], replicated, may hold values from 0 to 63
- j_batch: int32 [4], replicated, may hold values from 0 to 63
Outputs:
- residual: float32 [4, 608, 4, 608], P(None, 'blk', None, 'int')
Inputs may be any that keep to these rules, and one draw needn't show every extreme that they name: `occ_irrep`: labels of the eight D2h irreps; the product of two irreps is the bitwise exclusive or of their labels. `virt_irrep`: labels of the eight D2h irreps, combined as above; no irrep labels more than 96 virtual orbitals, and one labels exactly 96. `i_batch`: positions among the 64 occupied orbitals. `j_batch`: positions among the 64 occupied orbitals.
All inputs are finite; a program needn't handle non-finite values.
Results may differ from a plain program's by a relative error of at most 0.00007.
Values sent between devices are 32-bit elements; how exact they have to be, the bound alone decides.
A program may use at most 128 MiB of HBM per device.

v0:
```python
import jax
import jax.numpy as jnp
from jax import lax
from jax.sharding import PartitionSpec as P


def lookup(labels, where_at):
    positions = jnp.arange(labels.shape[0], dtype=jnp.int32)
    onehot = (where_at[:, None] == positions[None, :]).astype(jnp.int32)
    return jnp.sum(onehot * labels[None, :], axis=1)


def per_device(amplitudes, integrals, occ_irrep, virt_irrep, i_batch, j_batch):
    a_count = amplitudes.shape[1]
    k_count = amplitudes.shape[2]
    a_start = lax.axis_index("blk") * a_count
    k_start = lax.axis_index("int") * k_count
    occ_k = lax.dynamic_slice_in_dim(occ_irrep, k_start, k_count)
    virt_a = lax.dynamic_slice_in_dim(virt_irrep, a_start, a_count)
    irr_i = lookup(occ_irrep, i_batch)
    irr_j = lookup(occ_irrep, j_batch)
    left_pair = jnp.bitwise_xor(irr_i[:, None, None, None], occ_k[None, None, :, None])
    amp_keep = left_pair == jnp.bitwise_xor(
        virt_a[None, :, None, None], virt_irrep[None, None, None, :]
    )
    swap_keep = left_pair == jnp.bitwise_xor(
        virt_irrep[None, :, None, None], virt_a[None, None, None, :]
    )
    sym_amp = jnp.where(amp_keep, amplitudes, 0.0)
    moved = lax.all_to_all(amplitudes, "blk", split_axis=3, concat_axis=1, tiled=True)
    sym_moved = jnp.where(swap_keep, moved, 0.0)
    occ_virt = jnp.bitwise_xor(occ_k[:, None, None, None], virt_irrep[None, :, None, None])
    int_keep = occ_virt == jnp.bitwise_xor(
        irr_j[None, None, :, None], virt_irrep[None, None, None, :]
    )
    sym_piece = jnp.where(int_keep, lax.all_gather(integrals, "blk", axis=3, tiled=True), 0.0)
    cycle = jnp.einsum("iakc,kcjb->iajb", sym_amp, sym_piece, precision=lax.Precision.HIGHEST)
    swapped = jnp.einsum("icka,kcjb->iajb", sym_moved, sym_piece, precision=lax.Precision.HIGHEST)
    terms = jnp.stack((cycle, swapped))
    summed = lax.psum_scatter(terms, "int", scatter_dimension=4, tiled=True)
    return 2.0 * summed[0] - summed[1]


def solution(mesh):
    placed = (P(None, "blk", "int", None), P("int", None, None, "blk"), P(), P(), P(), P())
    return jax.shard_map(
        per_device,
        mesh=mesh,
        in_specs=placed,
        out_specs=P(None, "blk", None, "int"),
        check_vma=False,
    )
```

profile of v0, /device:TPU:2, one launch (start us, length us, event | category | flops | bytes accessed | tf_op | source)
XLA Modules:
  0.0 368.6 jit_solution(17444483353083959431)
XLA Ops:
  6.5 0.0 all-gather.2.cloned.1.call-start
  6.5 0.7 all-gather.2.cloned.1.call-update
  7.3 4.9 %copy.50 = f32[4,19,4,608]{1,2,0,3:T(4,128)} copy(f32[4,19,4,608]{3,2,1,0:T(4,128)} %param.6) | data formatting | bytes 1478656 | tf_op args[0]
  12.1 7.6 %reshape.168 = f32[32,1,5776]{2,1,0:T(1,128)} reshape(f32[608,4,4,19]{3,2,1,0:T(4,128)} %bitcast.42) | data formatting | bytes 1478656
  19.8 9.5 %all-to-all-start = ((f32[32,1,5776]{2,1,0:T(1,128)}), f32[32,1,5776]{2,1,0:T(1,128)S(1)}, u32[]{:S(2)}, u32[]{:S(2)}) async-start(f32[32,1,5776]{2,1,0:T(1,128)} %reshape.168), calls=%async_computation | async-start | bytes 1507328 | tf_op jit(solution)/shard_map/all_to_all | solution.py:30
  29.2 0.0 all-reduce.3.cloned.1.call-start
  29.3 0.7 dynamic_slice.6
  30.0 0.9 select_reduce_fusion.1
  30.9 0.8 broadcast_xor_fusion.3
  31.7 0.2 copy.47
  31.9 0.8 dynamic_slice.7
  32.6 0.1 broadcast_xor_fusion.4
  32.7 0.8 broadcast_xor_fusion
  33.5 0.8 broadcast_xor_fusion.1
  34.2 1.4 select_bitcast_fusion.1
  35.7 10.2 %all-to-all-done = f32[32,1,5776]{2,1,0:T(1,128)S(1)} async-done(((f32[32,1,5776]{2,1,0:T(1,128)}), f32[32,1,5776]{2,1,0:T(1,128)S(1)}, u32[]{:S(2)}, u32[]{:S(2)}) %all-to-all-start) | async-done | bytes 739360 | tf_op jit(solution)/shard_map/all_to_all | solution.py:30
  45.9 0.5 broadcast.124
  46.4 2.4 reduce
  48.9 8.0 %reshape.169 = f32[608,4,4,19]{3,2,1,0:T(4,128)} reshape(f32[32,5776]{1,0:T(8,128)S(1)} %reduce) | data formatting | bytes 1478656
  56.9 6.2 %copy.73 = f32[4,19,4,32,19]{1,3,2,4,0:T(8,128)} copy(f32[4,19,4,32,19]{1,2,0,4,3:T(4,128)} %bitcast.40) | data formatting | bytes 1478656 | tf_op jit(solution)/shard_map/all_to_all | solution.py:30
  63.1 6.0 %all_to_all.16 = f32[4,608,4,19]{1,2,3,0:T(4,128)S(1)} reshape(f32[4,32,19,4,19]{2,1,3,4,0:T(8,128)} %bitcast.41) | data formatting | bytes 1478656 | tf_op jit(solution)/shard_map/all_to_all | solution.py:30
  69.1 0.3 select_bitcast_fusion
  69.4 57.0 %all-gather.2.cloned.1.call-done = f32[4,608,4,608]{1,2,3,0:T(4,128)} async-done(((f32[4,608,4,19]{1,2,3,0:T(4,128)}), f32[4,608,4,608]{1,2,3,0:T(4,128)}) %all-gather.2.cloned.1.call-update) | async-done | bytes 23658512 | tf_op jit(solution)/shard_map/all_gather | solution.py:36
  126.3 22.7 %compare_select_fusion = f32[4,608,4,608]{1,2,3,0:T(4,128)} fusion(f32[4,608,4,608]{1,2,3,0:T(4,128)} %all-gather.2.cloned.1.call-done, s32[4,608]{0,1:T(8,128)S(1)} %copy.47, s32[4,608]{1,0:T(4,128)S(1)} %get-tuple-element.7), kind=kLoop, calls=%fused_computation.4 | loop fusion | flops 11829248 | bytes 47336448 | tf_op jit(solution)/shard_map/jit(_where)/select_n | solution.py:36
  149.0 30.2 %copy.49 = f32[4,608,4,608]{3,1,0,2:T(8,128)} copy(f32[4,608,4,608]{1,2,3,0:T(4,128)} %compare_select_fusion) | data formatting | bytes 47316992 | tf_op jit(solution)/shard_map/jit(_where)/select_n | solution.py:36
  179.2 18.0 %fusion.7 = f32[1,4,19,4,608]{4,2,3,1,0:T(8,128)S(1)} fusion(f32[4,608,4,608]{3,1,0,2:T(8,128)} %copy.49, f32[4,608,4,19,1]{1,2,3,0,4:T(4,128)S(1)} %select_bitcast_fusion), kind=kOutput, calls=%fused_computation.8 | convolution fusion | flops 5394137088 | bytes 25137152 | tf_op jit(solution)/shard_map/icka,kcjb->iajb/dot_general | solution.py:38
  197.3 18.1 %fusion.4 = f32[1,4,19,4,608]{4,2,3,1,0:T(8,128)S(1)} fusion(f32[4,608,4,608]{3,1,0,2:T(8,128)} %copy.49, f32[4,19,4,608,1]{3,2,1,0,4:T(4,128)S(1)} %select_bitcast_fusion.1), kind=kOutput, calls=%fused_computation.7 | convolution fusion | flops 5394137088 | bytes 25137152 | tf_op jit(solution)/shard_map/iakc,kcjb->iajb/dot_general | solution.py:37
  215.4 1.4 pad_maximum_fusion
  216.8 0.0 all-reduce.3.cloned.1.call-update
  216.8 1.3 dynamic-slice
  218.7 141.1 %all-reduce.3.cloned.1.call-done = f32[2,4,19,4,608]{4,2,3,1,0:T(8,128)} async-done(((f32[2,4,19,4,608]{4,2,3,1,0:T(8,128)}), f32[2,4,19,4,608]{4,2,3,1,0:T(8,128)}) %all-reduce.3.cloned.1.call-update) | async-done | bytes 1478672
  359.8 1.3 fusion.12
  361.1 0.7 copy.55
Async XLA Ops:
  6.5 119.8 %all-gather.2.cloned.1.call-start = ((), (), s32[]{:S(2)}) async-start(), calls=%async_computation.1 | async-start | bytes 25681920 | tf_op jit(solution)/shard_map/all_gather | solution.py:36
  19.8 26.2 %all-to-all-start = ((f32[32,1,5776]{2,1,0:T(1,128)}), f32[32,1,5776]{2,1,0:T(1,128)S(1)}, u32[]{:S(2)}, u32[]{:S(2)}) async-start(f32[32,1,5776]{2,1,0:T(1,128)} %reshape.168), calls=%async_computation | async-start | bytes 1507328 | tf_op jit(solution)/shard_map/all_to_all | solution.py:30
  29.2 330.6 %all-reduce.3.cloned.1.call-start = ((), (), s32[]{:S(2)}) async-start(), calls=%async_computation.2 | async-start | bytes 3932160
Sparse Core Ops, SparseCore 0:
  10.6 115.7 all-gather.1
  216.9 142.8 all-reduce.2
where the time goes:
time: 370 us; the launch traced here: 369 us
  waiting for transfers between devices  209 us (56%)
  local copies, waits for them, and re-layouts  67.1 us (18%)
  matrix products  36.1 us (10%)
  other arithmetic  32.8 us (9%)
  between operations  14.1 us (4%)
  starting transfers between devices  9.52 us (3%)
    unnamed x3, waiting for transfers between devices  142 us
    all_gather x1, waiting for transfers between devices, per_device(): lax.all_gather(integrals, 'blk', axis=3, tiled=True)  57 us
    select_n x1, local copies, waits for them, and re-layouts, per_device(): jnp.where(int_keep, lax.all_gather(integrals, 'blk', axis=3, tiled=True),...  30.2 us
    select_n x1, other arithmetic, per_device(): jnp.where(int_keep, lax.all_gather(integrals, 'blk', axis=3, tiled=True),...  22.7 us
    unnamed x4, local copies, waits for them, and re-layouts  21.8 us
    dot_general x1, matrix products, per_device(): jnp.einsum('iakc,kcjb->iajb', sym_amp, sym_piece, precision=lax.Precision...  18.1 us
    dot_general x1, matrix products, per_device(): jnp.einsum('icka,kcjb->iajb', sym_moved, sym_piece, precision=lax.Precisi...  18 us
    all_to_all x3, local copies, waits for them, and re-layouts, per_device(): lax.all_to_all(amplitudes, 'blk', split_axis=3, concat_axis=1, tiled=True)  12.7 us
  transfers between devices with their start and end apart: 3, of which 3 were waited for; matrix products, arithmetic and copies ran while one was open for 10% of the time, Pallas kernels for 0%

commit v1 on v0

--- a/solution.py
+++ b/solution.py
@@ -33,7 +33,12 @@
     int_keep = occ_virt == jnp.bitwise_xor(
         irr_j[None, None, :, None], virt_irrep[None, None, None, :]
     )
-    sym_piece = jnp.where(int_keep, lax.all_gather(integrals, "blk", axis=3, tiled=True), 0.0)
+
+    def outputs_read(where_dim, net_axis, unit):
+        x_next = jnp.stack([unit] * lax.axis_size(net_axis), 0)
+        return jnp.concatenate(lax.all_to_all(x_next, net_axis, 0, 0), where_dim)
+
+    sym_piece = jnp.where(int_keep, outputs_read(3, "blk", integrals), 0.0)
     cycle = jnp.einsum("iakc,kcjb->iajb", sym_amp, sym_piece, precision=lax.Precision.HIGHEST)
     swapped = jnp.einsum("icka,kcjb->iajb", sym_moved, sym_piece, precision=lax.Precision.HIGHEST)
     terms = jnp.stack((cycle, swapped))

time: 370 us -> 619 us (1.67)
  waiting for transfers between devices: 209 us -> 433 us
  blocking collectives: 0 us -> 21.6 us
  local copies, waits for them, and re-layouts: 67.1 us -> 88.1 us
  other arithmetic: 32.8 us -> 18.5 us
    all_to_all x1, waiting for transfers between devices: 10.2 us -> 285 us  [outputs_read(): return jnp.concatenate(lax.all_to_all(x_next, net_axis, 0, 0), where_dim)]
    all_gather x1 -> x0, waiting for transfers between devices: 57 us -> none  [per_device(): lax.all_gather(integrals, 'blk', axis=3, tiled=True)]
    all_to_all x0 -> x1, blocking collectives: none -> 21.6 us  [per_device(): lax.all_to_all(amplitudes, 'blk', split_axis=3, concat_axis=1, tiled=True)]
    reshape x0 -> x1, local copies, waits for them, and re-layouts: none -> 13.2 us  [outputs_read(): return jnp.concatenate(lax.all_to_all(x_next, net_axis, 0, 0), where_dim)]
    select_n x1, other arithmetic: 22.7 us -> 12.4 us  [per_device(): sym_piece = jnp.where(int_keep, outputs_read(3, 'blk', integrals), 0.0)]
    another operation x0 -> x1, local copies, waits for them, and re-layouts: none -> 9.87 us  [outputs_read(): x_next = jnp.stack([unit] * lax.axis_size(net_axis), 0)]
    unnamed x3 -> x2, waiting for transfers between devices: 142 us -> 148 us
    unnamed x4 -> x14, local copies, waits for them, and re-layouts: 21.8 us -> 21.2 us
  transfers between devices with their start and end apart: 3 -> 2, of which waited for: 3 -> 2; matrix products, arithmetic and copies ran while one was open for 10% -> 3% of each run, Pallas kernels for 0% -> 0%
where the time goes in v1:
time: 619 us; the launch traced here: 618 us
  waiting for transfers between devices  433 us (70%)
  local copies, waits for them, and re-layouts  88.1 us (14%)
  matrix products  36.1 us (6%)
  blocking collectives  21.6 us (3%)
  other arithmetic  18.5 us (3%)
  between operations  14.2 us (2%)
  starting transfers between devices  6.63 us (1%)
    all_to_all x1, waiting for transfers between devices, outputs_read(): return jnp.concatenate(lax.all_to_all(x_next, net_axis, 0, 0), where_dim)  285 us
    unnamed x2, waiting for transfers between devices  148 us
    select_n x1, local copies, waits for them, and re-layouts, per_device(): sym_piece = jnp.where(int_keep, outputs_read(3, 'blk', integrals), 0.0)  30.1 us
    all_to_all x1, blocking collectives, per_device(): lax.all_to_all(amplitudes, 'blk', split_axis=3, concat_axis=1, tiled=True)  21.6 us
    unnamed x14, local copies, waits for them, and re-layouts  21.2 us
    dot_general x1, matrix products, per_device(): jnp.einsum('iakc,kcjb->iajb', sym_amp, sym_piece, precision=lax.Precision...  18.1 us
    dot_general x1, matrix products, per_device(): jnp.einsum('icka,kcjb->iajb', sym_moved, sym_piece, precision=lax.Precisi...  18 us
    reshape x1, local copies, waits for them, and re-layouts, outputs_read(): return jnp.concatenate(lax.all_to_all(x_next, net_axis, 0, 0), where_dim)  13.2 us
  transfers between devices with their start and end apart: 2, of which 2 were waited for; matrix products, arithmetic and copies ran while one was open for 3% of the time, Pallas kernels for 0%

profile of v1, /device:TPU:2, one launch (start us, length us, event | category | flops | bytes accessed | tf_op | source)
XLA Modules:
  0.0 618.1 jit_solution(3457508126714796343)
XLA Ops:
  6.5 4.9 copy.52
  11.4 7.0 %reshape.178 = f32[32,1,5776]{2,1,0:T(1,128)S(1)} reshape(f32[608,4,4,19]{3,2,1,0:T(4,128)} %bitcast.45) | data formatting | bytes 1478656
  18.4 21.6 %all_to_all.23 = f32[32,1,5776]{2,1,0:T(1,128)S(1)} all-to-all(f32[32,1,5776]{2,1,0:T(1,128)S(1)} %reshape.178), channel_id=1, replica_groups=mesh['blk'=32,'int'=16] {'blk'}, dimensions={0} | all-to-all | bytes 1478656 | tf_op jit(solution)/shard_map/all_to_all | solution.py:30
  40.0 9.9 %stack.8 = f32[32,4,608,4,19]{2,3,4,1,0:T(4,128)} broadcast(f32[4,608,4,19]{1,2,3,0:T(4,128)} %param.7), dimensions={1,2,3,4} | broadcast | bytes 24397824 | tf_op jit(solution)/shard_map/stack | solution.py:38
  49.9 0.0 copy-start.2
  49.9 0.0 copy-start.3
  49.9 0.0 copy-start.4
  49.9 0.0 copy-start.1
  49.9 0.0 copy-start
  49.9 6.6 %all-to-all-start = ((f32[32,4,608,4,19]{2,3,4,1,0:T(4,128)}), f32[32,4,608,4,19]{2,3,4,1,0:T(4,128)}, u32[]{:S(2)}, u32[]{:S(2)}) async-start(f32[32,4,608,4,19]{2,3,4,1,0:T(4,128)} %stack.8), calls=%async_computation | async-start | bytes 49807360 | tf_op jit(solution)/shard_map/all_to_all | solution.py:39
  56.5 0.0 all-reduce.3.cloned.1.call-start
  56.5 0.0 copy-done.2
  56.5 0.1 dynamic_slice.6
  56.6 0.0 copy-done.3
  56.6 0.0 copy-done.4
  56.6 0.2 select_reduce_fusion.1
  56.8 0.0 copy-done.1
  56.9 0.1 broadcast_xor_fusion.3
  56.9 0.2 copy.48
  57.1 0.1 dynamic_slice.7
  57.2 0.1 broadcast_xor_fusion.4
  57.3 0.1 broadcast_xor_fusion
  57.3 0.1 broadcast_xor_fusion.1
  57.4 0.0 copy-done
  57.4 0.2 select_bitcast_fusion.1
  57.7 0.5 broadcast.126
  58.2 2.4 reduce
  60.6 8.0 %reshape.179 = f32[608,4,4,19]{3,2,1,0:T(4,128)} reshape(f32[32,5776]{1,0:T(8,128)S(1)} %reduce) | data formatting | bytes 1478656
  68.7 6.2 %copy.75 = f32[4,19,4,32,19]{1,3,2,4,0:T(8,128)} copy(f32[4,19,4,32,19]{1,2,0,4,3:T(4,128)} %bitcast.43) | data formatting | bytes 1478656 | tf_op jit(solution)/shard_map/all_to_all | solution.py:30
  74.9 6.0 all_to_all.20
  80.9 0.3 select_bitcast_fusion
  81.1 285.4 %all-to-all-done = f32[32,4,608,4,19]{2,3,4,1,0:T(4,128)} async-done(((f32[32,4,608,4,19]{2,3,4,1,0:T(4,128)}), f32[32,4,608,4,19]{2,3,4,1,0:T(4,128)}, u32[]{:S(2)}, u32[]{:S(2)}) %all-to-all-start) | async-done | bytes 23658528 | tf_op jit(solution)/shard_map/all_to_all | solution.py:39
  366.5 13.2 %copy.49 = f32[4,608,4,32,19]{1,2,4,3,0:T(4,128)S(1)} copy(f32[4,608,4,32,19]{1,2,4,0,3:T(4,128)} %bitcast.1) | data formatting | bytes 47316992 | tf_op jit(solution)/shard_map/reshape | solution.py:39
  379.8 12.4 %compare_select_fusion = f32[4,608,4,608]{1,2,3,0:T(4,128)} fusion(f32[4,608,4,608]{1,2,3,0:T(4,128)S(1)} %bitcast.42, s32[4,608]{0,1:T(8,128)S(1)} %copy.48, s32[4,608]{1,0:T(4,128)S(1)} %get-tuple-element.7), kind=kLoop, calls=%fused_computation.4 | loop fusion | flops 11829248 | bytes 47336448 | tf_op jit(solution)/shard_map/jit(_where)/select_n | solution.py:41
  392.2 30.1 %copy.51 = f32[4,608,4,608]{3,1,0,2:T(8,128)} copy(f32[4,608,4,608]{1,2,3,0:T(4,128)} %compare_select_fusion) | data formatting | bytes 47316992 | tf_op jit(solution)/shard_map/jit(_where)/select_n | solution.py:41
  422.3 18.0 %fusion.7 = f32[1,4,19,4,608]{4,2,3,1,0:T(8,128)S(1)} fusion(f32[4,608,4,608]{3,1,0,2:T(8,128)} %copy.51, f32[4,608,4,19,1]{1,2,3,0,4:T(4,128)S(1)} %select_bitcast_fusion), kind=kOutput, calls=%fused_computation.8 | convolution fusion | flops 5394137088 | bytes 25137152 | tf_op jit(solution)/shard_map/icka,kcjb->iajb/dot_general | solution.py:43
  440.3 18.1 %fusion.4 = f32[1,4,19,4,608]{4,2,3,1,0:T(8,128)S(1)} fusion(f32[4,608,4,608]{3,1,0,2:T(8,128)} %copy.51, f32[4,19,4,608,1]{3,2,1,0,4:T(4,128)S(1)} %select_bitcast_fusion.1), kind=kOutput, calls=%fused_computation.7 | convolution fusion | flops 5394137088 | bytes 25137152 | tf_op jit(solution)/shard_map/iakc,kcjb->iajb/dot_general | solution.py:42
  458.4 1.4 pad_maximum_fusion
  459.8 0.0 all-reduce.3.cloned.1.call-update
  459.8 1.3 dynamic-slice
  461.8 147.5 %all-reduce.3.cloned.1.call-done = f32[2,4,19,4,608]{4,2,3,1,0:T(8,128)} async-done(((f32[2,4,19,4,608]{4,2,3,1,0:T(8,128)}), f32[2,4,19,4,608]{4,2,3,1,0:T(8,128)}) %all-reduce.3.cloned.1.call-update) | async-done | bytes 1478672
  609.3 1.3 fusion.12
  610.5 0.7 copy.57
Async XLA Ops:
  49.9 6.7 %copy-start.2 = (s32[64]{0:T(128)S(1)}, s32[64]{0:T(128)}, u32[]{:S(2)}) copy-start(s32[64]{0:T(128)} %param.8) | copy-start | bytes 772
  49.9 6.8 %copy-start.3 = (s32[4]{0:T(128)S(1)}, s32[4]{0:T(128)}, u32[]{:S(2)}) copy-start(s32[4]{0:T(128)} %param.10) | copy-start | bytes 52
  49.9 6.8 %copy-start.4 = (s32[4]{0:T(128)S(1)}, s32[4]{0:T(128)}, u32[]{:S(2)}) copy-start(s32[4]{0:T(128)} %param.11) | copy-start | bytes 52
  49.9 7.0 %copy-start.1 = (s32[608]{0:T(1024)S(1)}, s32[608]{0:T(1024)}, u32[]{:S(2)}) copy-start(s32[608]{0:T(1024)} %param.9) | copy-start | bytes 7300
  49.9 7.5 %copy-start = (f32[4,19,4,608]{3,2,1,0:T(4,128)S(1)}, f32[4,19,4,608]{3,2,1,0:T(4,128)}, u32[]{:S(2)}) copy-start(f32[4,19,4,608]{3,2,1,0:T(4,128)} %param.6) | copy-start | bytes 2217988
  49.9 316.7 %all-to-all-start = ((f32[32,4,608,4,19]{2,3,4,1,0:T(4,128)}), f32[32,4,608,4,19]{2,3,4,1,0:T(4,128)}, u32[]{:S(2)}, u32[]{:S(2)}) async-start(f32[32,4,608,4,19]{2,3,4,1,0:T(4,128)} %stack.8), calls=%async_computation | async-start | bytes 49807360 | tf_op jit(solution)/shard_map/all_to_all | solution.py:39
  56.5 552.8 %all-reduce.3.cloned.1.call-start = ((), (), s32[]{:S(2)}) async-start(), calls=%async_computation.2 | async-start | bytes 3932160
Sparse Core Ops, SparseCore 0:
  460.0 149.2 all-reduce.2
